TPU v7x, 256 devices: a whole 4x4x8 slice. The times are simulated.
256 devices in a mesh: req: 4 (over z_hi, core), ctx: 64 (over x, y, z_lo).
Axes of the slice: x: 4, y: 4, z: 8 (z_hi: 2, z_lo: 4; z = z_hi * 4 + z_lo), core: 2. Of those that a mesh axis runs over, the one named last changes fastest.
Arguments:
- query_rows: bfloat16 [4, 7168, 2048], P('req', 'ctx'), may hold values from -120 to 120
- key_rows: bfloat16 [4, 7168, 1024], P('req', 'ctx'), may hold values from -8 to 8
- value_rows: bfloat16 [4, 7168, 1024], P('req', 'ctx'), may hold values from -6 to 6
- image_starts: int32 [4, 14], P('req'), may hold values from 0 to 6912, as said below
- image_counts: int32 [4], P('req'), may hold values from 1 to 14, as said below
Outputs:
- attended: bfloat16 [4, 7168, 2048], P('req', 'ctx')
Inputs may be any that keep to these rules, and one draw needn't show every extreme that they name: `image_starts`: each request's row holds 14 distinct multiples of 256 in ascending order, always starting with 0; in some request the last entry is (27) * 256; only the first image_counts entries of a request are image blocks. `image_counts`: some request has 14 image blocks.
All inputs are finite; a program needn't handle non-finite values.
Results may differ from a plain program's by a relative error of at most 0.0059.
Values may be sent and summed in bfloat16 or wider, within the bound.
A program may use at most 128 MiB of HBM per device.

v0:
```python
import jax
import jax.numpy as jnp
from jax import lax
from jax.sharding import PartitionSpec as P

HEADS = 16
KV_HEADS = 8
HEAD_DIM = 128
IMG = 256


score_scale = 168.0 ** (-0.5)


def image_ids(position, starts, count):
    index = jnp.arange(starts.shape[0], dtype=jnp.int32)
    inside = (
        (starts[None, :] <= position[:, None])
        & (position[:, None] < starts[None, :] + IMG)
        & (index[None, :] < count)
    )
    return jnp.sum(jnp.where(inside, index[None, :] + 1, 0), axis=1) - 1


def shards(query_rows, key_rows, value_rows, image_starts, image_counts):
    my_index = lax.axis_index("ctx")
    row_count = query_rows.shape[1]
    starts = image_starts[0]
    count = image_counts[0]
    local_pos = jnp.arange(row_count, dtype=jnp.int32)
    query_pos = my_index * row_count + local_pos
    query_ids = image_ids(query_pos, starts, count)
    group = HEADS // KV_HEADS
    query_heads = query_rows[0].reshape(row_count, KV_HEADS, group, HEAD_DIM)
    initial = (
        jnp.full((KV_HEADS, group, row_count), -1e30, jnp.float32),
        jnp.zeros((KV_HEADS, group, row_count), jnp.float32),
        jnp.zeros((KV_HEADS, group, row_count, HEAD_DIM), jnp.float32),
    )

    def add_block(state, key_block, value_block, key_pos):
        key_ids = image_ids(key_pos, starts, count)
        visible = (key_pos[None, :] <= query_pos[:, None]) | (
            key_ids[None, :] == query_ids[:, None]
        ) & (query_ids[:, None] >= 0)

        def update(carried):
            running_max, running_total, running_sum = carried
            scores = (
                jnp.einsum(
                    "qkgd,skd->kgqs", query_heads, key_block, preferred_element_type=jnp.float32
                )
                * score_scale
            )
            scores = jnp.where(visible[None, None], scores, -1e30)
            new_max = jnp.maximum(running_max, jnp.max(scores, axis=-1))
            factor = jnp.exp(running_max - new_max)
            weights = jnp.where(visible[None, None], jnp.exp(scores - new_max[..., None]), 0.0)
            new_total = running_total * factor + jnp.sum(weights, axis=-1)
            product = jnp.einsum(
                "kgqs,skd->kgqd",
                weights.astype(jnp.bfloat16),
                value_block,
                preferred_element_type=jnp.float32,
            )
            return (new_max, new_total, running_sum * factor[..., None] + product)

        return lax.cond(jnp.any(visible), update, lambda carried: carried, state)

    start = jnp.int32(0)
    key_piece = lax.all_gather(key_rows, "ctx", axis=1, tiled=True)
    value_piece = lax.all_gather(value_rows, "ctx", axis=1, tiled=True)
    piece_rows = key_piece.shape[1]
    block_rows = max(
        (size for size in range(1, min(piece_rows, 1024) + 1) if piece_rows % size == 0)
    )
    block_total = piece_rows // block_rows
    key_blocks = key_piece[0].reshape(block_total, block_rows, KV_HEADS, HEAD_DIM)
    value_blocks = value_piece[0].reshape(block_total, block_rows, KV_HEADS, HEAD_DIM)

    def scan_step(carried, items):
        key_block, value_block, block_index = items
        key_pos = start + block_index * block_rows + jnp.arange(block_rows, dtype=jnp.int32)
        return (add_block(carried, key_block, value_block, key_pos), None)

    result, unused = lax.scan(
        scan_step, initial, (key_blocks, value_blocks, jnp.arange(block_total, dtype=jnp.int32))
    )
    final_max, final_total, final_sum = result
    output = final_sum / final_total[..., None]
    output = output.transpose(2, 0, 1, 3).reshape(row_count, HEADS * HEAD_DIM).astype(jnp.bfloat16)
    return output[None]


def solution(mesh):
    return jax.shard_map(
        shards,
        mesh=mesh,
        in_specs=(
            P("req", "ctx", None),
            P("req", "ctx", None),
            P("req", "ctx", None),
            P("req", None),
            P("req"),
        ),
        out_specs=P("req", "ctx", None),
        check_vma=False,
    )
```

profile of v0, /device:TPU:126, one launch (start us, length us, event | category | flops | bytes accessed | tf_op | source)
XLA Modules:
  0.0 935.1 jit_solution(16546968612578805428)
XLA Ops:
  6.5 0.7 all-gather.3.cloned.1.call-update
  7.3 0.7 all-gather.5.cloned.1.call-update
  8.7 1.3 reshape_squeeze.10
  10.8 0.7 select_reduce_fusion.1
  11.6 402.7 %all-gather.3.cloned.1.call-done = bf16[1,7168,1024]{2,1,0:T(8,128)(2,1)} async-done(((bf16[1,112,1024]{2,1,0:T(8,128)(2,1)}), bf16[1,7168,1024]{2,1,0:T(8,128)(2,1)}) %all-gather.3.cloned.1.call-update) | async-done | bytes 14680080 | tf_op jit(solution)/shard_map/all_gather | solution.py:71
  414.3 9.1 copy.17
  423.5 6.5 copy.11
  430.0 388.6 %all-gather.5.cloned.1.call-done = bf16[1,7168,1024]{2,1,0:T(8,128)(2,1)} async-done(((bf16[1,112,1024]{2,1,0:T(8,128)(2,1)}), bf16[1,7168,1024]{2,1,0:T(8,128)(2,1)}) %all-gather.5.cloned.1.call-update) | async-done | bytes 14680080 | tf_op jit(solution)/shard_map/all_gather | solution.py:72
  818.6 9.1 copy.18
  827.7 6.4 copy.13
  834.2 92.3 %while.17 = (s32[]{:T(128)}, f32[8,2,112]{2,1,0:T(2,128)S(1)}, f32[8,2,112]{2,1,0:T(2,128)S(1)}, f32[8,2,112,128]{3,2,1,0:T(8,128)S(1)}, s32[7]{0:T(128)S(1)}, /...) while((s32[]{:T(128)}, f32[8,2,112]{2,1,0:T(2,128)S(1)}, ...), condition=%wide.region_8.9_spmd.clone, body=%wide.region_1.8_spmd.clone.sunk | while | flops 964502272 | bytes 29113972 | solution.py:86
  836.4 0.9 fusion.27
  838.0 9.4 %conditional.3 = ((f32[8,2,112]{2,1,0:T(2,128)S(1)}, f32[8,2,112]{2,1,0:T(2,128)S(1)}, f32[8,2,112,128]{3,2,1,0:T(8,128)S(1)})) conditional(s32[]{:T(128)} %convert_element_type.39, (f32[8,2,112]{2,1,0:T(2,128)S(1)}, f32[8,2,112]{2,1,0:T(2,128)S(1)}, f32[8,2,112,128]{3,2,1,0:T(8,128)S(1)}) %tuple.57, (pred[112,1024]{1,0:T(8,128)(4,1)S(1)}, ...), branch_computations={%region_4.4_spmd, %region_5.7_spmd} | conditional | flops 963841536 | bytes 28967968 | solution.py:68
  838.0 3.0 fusion.2
  841.1 2.4 fusion.4
  843.5 3.9 fusion.13
  847.4 0.7 dynamic_slice.40
  849.6 0.9 fusion.27
  851.2 9.4 %conditional.3 = ((f32[8,2,112]{2,1,0:T(2,128)S(1)}, f32[8,2,112]{2,1,0:T(2,128)S(1)}, f32[8,2,112,128]{3,2,1,0:T(8,128)S(1)})) conditional(s32[]{:T(128)} %convert_element_type.39, (f32[8,2,112]{2,1,0:T(2,128)S(1)}, f32[8,2,112]{2,1,0:T(2,128)S(1)}, f32[8,2,112,128]{3,2,1,0:T(8,128)S(1)}) %tuple.57, (pred[112,1024]{1,0:T(8,128)(4,1)S(1)}, ...), branch_computations={%region_4.4_spmd, %region_5.7_spmd} | conditional | flops 963841536 | bytes 28967968 | solution.py:68
  851.2 3.0 fusion.2
  854.3 2.4 fusion.4
  856.7 3.9 fusion.13
  862.8 0.9 fusion.27
  864.4 9.4 %conditional.3 = ((f32[8,2,112]{2,1,0:T(2,128)S(1)}, f32[8,2,112]{2,1,0:T(2,128)S(1)}, f32[8,2,112,128]{3,2,1,0:T(8,128)S(1)})) conditional(s32[]{:T(128)} %convert_element_type.39, (f32[8,2,112]{2,1,0:T(2,128)S(1)}, f32[8,2,112]{2,1,0:T(2,128)S(1)}, f32[8,2,112,128]{3,2,1,0:T(8,128)S(1)}) %tuple.57, (pred[112,1024]{1,0:T(8,128)(4,1)S(1)}, ...), branch_computations={%region_4.4_spmd, %region_5.7_spmd} | conditional | flops 963841536 | bytes 28967968 | solution.py:68
  864.4 3.0 fusion.2
  867.4 2.4 fusion.4
  869.8 3.9 fusion.13
  875.9 0.9 fusion.27
  877.6 9.4 %conditional.3 = ((f32[8,2,112]{2,1,0:T(2,128)S(1)}, f32[8,2,112]{2,1,0:T(2,128)S(1)}, f32[8,2,112,128]{3,2,1,0:T(8,128)S(1)})) conditional(s32[]{:T(128)} %convert_element_type.39, (f32[8,2,112]{2,1,0:T(2,128)S(1)}, f32[8,2,112]{2,1,0:T(2,128)S(1)}, f32[8,2,112,128]{3,2,1,0:T(8,128)S(1)}) %tuple.57, (pred[112,1024]{1,0:T(8,128)(4,1)S(1)}, ...), branch_computations={%region_4.4_spmd, %region_5.7_spmd} | conditional | flops 963841536 | bytes 28967968 | solution.py:68
  877.6 3.0 fusion.2
  880.6 2.4 fusion.4
  883.0 3.9 fusion.13
  889.1 0.9 fusion.27
  890.7 9.4 %conditional.3 = ((f32[8,2,112]{2,1,0:T(2,128)S(1)}, f32[8,2,112]{2,1,0:T(2,128)S(1)}, f32[8,2,112,128]{3,2,1,0:T(8,128)S(1)})) conditional(s32[]{:T(128)} %convert_element_type.39, (f32[8,2,112]{2,1,0:T(2,128)S(1)}, f32[8,2,112]{2,1,0:T(2,128)S(1)}, f32[8,2,112,128]{3,2,1,0:T(8,128)S(1)}) %tuple.57, (pred[112,1024]{1,0:T(8,128)(4,1)S(1)}, ...), branch_computations={%region_4.4_spmd, %region_5.7_spmd} | conditional | flops 963841536 | bytes 28967968 | solution.py:68
  890.8 3.0 fusion.2
  893.8 2.4 fusion.4
  896.2 3.9 fusion.13
  902.3 0.9 fusion.27
  903.9 9.4 %conditional.3 = ((f32[8,2,112]{2,1,0:T(2,128)S(1)}, f32[8,2,112]{2,1,0:T(2,128)S(1)}, f32[8,2,112,128]{3,2,1,0:T(8,128)S(1)})) conditional(s32[]{:T(128)} %convert_element_type.39, (f32[8,2,112]{2,1,0:T(2,128)S(1)}, f32[8,2,112]{2,1,0:T(2,128)S(1)}, f32[8,2,112,128]{3,2,1,0:T(8,128)S(1)}) %tuple.57, (pred[112,1024]{1,0:T(8,128)(4,1)S(1)}, ...), branch_computations={%region_4.4_spmd, %region_5.7_spmd} | conditional | flops 963841536 | bytes 28967968 | solution.py:68
  903.9 3.0 fusion.2
  907.0 2.4 fusion.4
  909.4 3.9 fusion.13
  915.5 0.9 fusion.27
  917.1 9.4 %conditional.3 = ((f32[8,2,112]{2,1,0:T(2,128)S(1)}, f32[8,2,112]{2,1,0:T(2,128)S(1)}, f32[8,2,112,128]{3,2,1,0:T(8,128)S(1)})) conditional(s32[]{:T(128)} %convert_element_type.39, (f32[8,2,112]{2,1,0:T(2,128)S(1)}, f32[8,2,112]{2,1,0:T(2,128)S(1)}, f32[8,2,112,128]{3,2,1,0:T(8,128)S(1)}) %tuple.57, (pred[112,1024]{1,0:T(8,128)(4,1)S(1)}, ...), branch_computations={%region_4.4_spmd, %region_5.7_spmd} | conditional | flops 963841536 | bytes 28967968 | solution.py:68
  917.1 3.0 fusion.2
  920.2 2.4 fusion.4
  922.6 3.9 fusion.13
  927.2 1.1 convert_element_type.29
  (92 shorter events, 11.1 us)
Async XLA Ops:
  6.5 407.8 %all-gather.3.cloned.1.call-start = ((), (), s32[]{:S(2)}) async-start(), calls=%async_computation | async-start | bytes 14909440 | tf_op jit(solution)/shard_map/all_gather | solution.py:71
  7.3 811.3 %all-gather.5.cloned.1.call-start = ((), (), s32[]{:S(2)}) async-start(), calls=%async_computation.1 | async-start | bytes 14909440 | tf_op jit(solution)/shard_map/all_gather | solution.py:72
  827.7 6.5 copy-start
Sparse Core Ops, SparseCore 0:
  9.1 405.1 all-gather.2
  416.1 402.4 all-gather.4
where the time goes:
time: 936 us; the launch traced here: 935 us
  waiting for transfers between devices  793 us (85%)
  matrix products  48.3 us (5%)
  local copies, waits for them, and re-layouts  38.8 us (4%)
  other arithmetic  30.4 us (3%)
  between operations  14.2 us (2%)
  loops' own time  10.6 us (1%)
    all_gather x1, waiting for transfers between devices, shards(): key_piece = lax.all_gather(key_rows, 'ctx', axis=1, tiled=True)  403 us
    all_gather x1, waiting for transfers between devices, shards(): value_piece = lax.all_gather(value_rows, 'ctx', axis=1, tiled=True)  389 us
    unnamed x7, local copies, waits for them, and re-layouts  31.3 us
    dot_general x7, matrix products, update(): jnp.einsum('kgqs,skd->kgqd', weights.astype(jnp.bfloat16), value_block, p...  27.2 us
    dot_general x7, matrix products, update(): jnp.einsum('qkgd,skd->kgqs', query_heads, key_block, preferred_element_ty...  21.2 us
  transfers between devices with their start and end apart: 2, of which 2 were waited for; matrix products, arithmetic and copies ran while one was open for 2% of the time, Pallas kernels for 0%

commit v1 on v0

v1 whole, which is shorter than its diff:
```python
import functools
import math

import jax
import jax.numpy as jnp
from jax import lax
from jax.experimental import pallas as pl
from jax.experimental.pallas import tpu as pltpu
from jax.sharding import PartitionSpec as P

HEADS = 16
KV_HEADS = 8
HEAD_DIM = 128
IMG = 256
SIDE = 4
PLANE = SIDE * SIDE
GROUP = HEADS // KV_HEADS
WIDE = GROUP * HEAD_DIM
NEG = -1e30
MESH = pl.DeviceIdType.MESH

score_scale = 168.0 ** (-0.5)
EXP2_SCALE = score_scale * math.log2(math.e)


def place(x, y, z):
    return {"ctx": x * PLANE + y * SIDE + z}


def kernel(starts_ref, count_ref, q_ref, k_ref, v_ref, out_ref,
           qg, kv, lim, acc, mx, sm, osend, ssend, orecv, srecv,
           q_ss, q_rs, p_ss, p_rs, up_ss, dn_ss, z_rs, o_ss, o_rs, s_ss, s_rs):
    rows = q_ref.shape[0]
    maximg = starts_ref.shape[1]
    c = lax.axis_index("ctx")
    x, y, z = c // PLANE, (c // SIDE) % SIDE, c % SIDE
    half = ((y + 1) // 2) % 2
    hb = y // 2
    mine = x * SIDE + y

    barrier = pltpu.get_barrier_semaphore()
    for dx in range(SIDE):
        for dy in range(SIDE):
            if dx or dy:
                pl.semaphore_signal(barrier, inc=1, device_id=place((x + dx) % SIDE, (y + dy) % SIDE, z), device_id_type=MESH)

    @pl.when(z < SIDE - 1)
    def _():
        pl.semaphore_signal(barrier, inc=1, device_id=place(x, y, z + 1), device_id_type=MESH)

    @pl.when(z > 0)
    def _():
        pl.semaphore_signal(barrier, inc=1, device_id=place(x, y, z - 1), device_id_type=MESH)

    inner = ((z > 0) & (z < SIDE - 1)).astype(jnp.int32)
    pl.semaphore_wait(barrier, PLANE - 1 + 1 + inner)

    def cols(n, width):
        return pl.ds(pl.multiple_of(n * width, width), width)

    p_sends = []
    for dx in range(SIDE):
        for j in range(2):
            tx = (x + dx) % SIDE
            ty = y if j == 0 else SIDE - 1 - y
            th = 2 * tx + (hb if j == 0 else 1 - hb)
            for t, ref in enumerate((k_ref, v_ref)):
                src = ref.at[:, cols(th, HEAD_DIM)]
                dst = kv.at[x, t, hb, z]
                n = (dx * 2 + j) * 2 + t
                if dx == 0 and j == 0:
                    pltpu.make_async_copy(src, dst, p_rs.at[t, x, hb]).start()
                else:
                    copy = pltpu.make_async_remote_copy(
                        src_ref=src, dst_ref=dst, send_sem=p_ss.at[n], recv_sem=p_rs.at[t, x, hb],
                        device_id=place(tx, ty, z), device_id_type=MESH)
                    copy.start()
                    p_sends.append(copy)
    q_sends = []
    for dx in range(SIDE):
        for dy in range(SIDE):
            tx, ty = (x + dx) % SIDE, (y + dy) % SIDE
            th = 2 * tx + ty // 2
            src = q_ref.at[:, cols(th, WIDE)]
            dst = qg.at[mine]
            if dx == 0 and dy == 0:
                pltpu.make_async_copy(src, dst, q_rs.at[mine]).start()
            else:
                copy = pltpu.make_async_remote_copy(
                    src_ref=src, dst_ref=dst, send_sem=q_ss.at[dx * SIDE + dy], recv_sem=q_rs.at[mine],
                    device_id=place(tx, ty, z), device_id_type=MESH)
                copy.start()
                q_sends.append(copy)

    def z_copy(xk, zk, step, ss):
        return pltpu.make_async_remote_copy(
            src_ref=kv.at[xk, :, :, zk], dst_ref=kv.at[xk, :, :, zk], send_sem=ss.at[xk, zk], recv_sem=z_rs.at[xk, zk],
            device_id=place(x, y, (z + step + SIDE) % SIDE), device_id_type=MESH)

    def send_up(xk, zk):
        @pl.when(z < SIDE - 1)
        def _():
            z_copy(xk, zk, 1, up_ss).start()

    def send_down(xk, zk):
        @pl.when(z > 0)
        def _():
            z_copy(xk, zk, -1, dn_ss).start()

    for xk in range(SIDE):
        for hk in range(2):
            for t in range(2):
                pltpu.make_async_copy(kv.at[xk, t, hk, z], kv.at[xk, t, hk, z], p_rs.at[t, xk, hk]).wait()
        send_up(xk, z)
        send_down(xk, z)

    def limits(i, carry):
        pos = (i * SIDE + z) * rows + lax.broadcasted_iota(jnp.int32, (rows, HEAD_DIM), 0)
        slot = pos // IMG * IMG
        found = jnp.zeros((rows, HEAD_DIM), jnp.int32)
        for n in range(maximg):
            first = jnp.where(n < count_ref[0], starts_ref[0, n], -1)
            found = jnp.where(slot == first, 1, found)
        lim[i] = jnp.where(found > 0, slot + (IMG - 1), pos)
        return carry

    lax.fori_loop(0, PLANE, limits, 0)

    def arrived(xk, zk):
        z_copy(xk, zk, 0, up_ss).wait_recv()

    @pl.when(inner > 0)
    def _():
        for d in range(1, SIDE):
            for xk in range(SIDE):
                @pl.when(z - d >= 0)
                def _():
                    arrived(xk, z - d)
                    send_up(xk, z - d)

                @pl.when(z + d <= SIDE - 1)
                def _():
                    arrived(xk, z + d)
                    send_down(xk, z + d)

    for i in range(PLANE):
        pltpu.make_async_copy(qg.at[i], qg.at[i], q_rs.at[i]).wait()

    keys = 2 * SIDE * rows
    y_low = half
    y_high = SIDE - 1 - half

    def tile(i, xk, masked):
        qq = qg[i]
        q = jnp.concatenate([qq[:, :HEAD_DIM], qq[:, HEAD_DIM:]], axis=0)
        k = kv[xk, 0].reshape(keys, HEAD_DIM)
        v = kv[xk, 1].reshape(keys, HEAD_DIM)
        s = lax.dot_general(q, k, (((1,), (1,)), ((), ())), preferred_element_type=jnp.float32)
        if masked:
            at = lax.broadcasted_iota(jnp.int32, (1, keys), 1)
            kpos = (xk * PLANE * rows) + at + jnp.where(at < keys // 2, y_low, y_high - 1) * (keys // 2)
            row_lim = lim[i]
            row_lim = jnp.concatenate([row_lim, row_lim], axis=0)[:, :1]
            seen = kpos <= row_lim
            s = jnp.where(seen, s, NEG)
        top = jnp.max(s, axis=1, keepdims=True)
        if xk > 0:
            before = mx[i][:, :1]
            top = jnp.maximum(top, before)
            shrink = jnp.exp2((before - top) * EXP2_SCALE)
        p = jnp.exp2((s - top) * EXP2_SCALE)
        if masked and xk == 0:
            p = jnp.where(seen, p, 0.0)
        total = jnp.sum(p, axis=1, keepdims=True)
        o = jnp.dot(p.astype(jnp.bfloat16), v, preferred_element_type=jnp.float32)
        if xk > 0:
            total = total + sm[i][:, :1] * shrink
            o = o + acc[i] * shrink
        if not masked:
            mx[i] = jnp.broadcast_to(top, (GROUP * rows, HEAD_DIM))
            sm[i] = jnp.broadcast_to(total, (GROUP * rows, HEAD_DIM))
            acc[i] = o
        else:
            o = (o / jnp.maximum(total, 1e-30)).astype(jnp.bfloat16)
            osend[i] = jnp.concatenate([o[:rows], o[rows:]], axis=1)
            lane = lax.broadcasted_iota(jnp.int32, (rows, HEAD_DIM), 1)
            stats = jnp.where(lane == 0, top[:rows], jnp.where(lane == 1, total[:rows], jnp.where(
                lane == 2, top[rows:], total[rows:])))
            stats = jnp.concatenate([stats, jnp.zeros((HEAD_DIM - rows, HEAD_DIM), jnp.float32)], axis=0)
            ssend[i] = stats.T[:8]

    def out_copies(xq, dy):
        ty = (y + dy) % SIDE
        i = xq * SIDE + ty
        to = place(xq, ty, z)
        a = pltpu.make_async_remote_copy(src_ref=osend.at[i], dst_ref=orecv.at[mine], send_sem=o_ss.at[xq, dy],
                                         recv_sem=o_rs.at[mine], device_id=to, device_id_type=MESH)
        b = pltpu.make_async_remote_copy(src_ref=ssend.at[i], dst_ref=srecv.at[mine], send_sem=s_ss.at[xq, dy],
                                         recv_sem=s_rs.at[mine], device_id=to, device_id_type=MESH)
        return a, b

    for xk in range(SIDE):
        @pl.when(z == 0)
        def _():
            for d in range(1, SIDE):
                arrived(xk, d)

        @pl.when(z == SIDE - 1)
        def _():
            for d in range(1, SIDE):
                arrived(xk, SIDE - 1 - d)

        def last(n, carry):
            tile(xk * SIDE + n, xk, True)
            return carry

        def more(n, carry):
            tile(n, xk, False)
            return carry

        lax.fori_loop(0, SIDE, last, 0)
        for dy in range(SIDE):
            own = (xk == x) if dy == 0 else None
            if dy == 0:
                @pl.when(x == xk)
                def _():
                    pltpu.make_async_copy(osend.at[mine], orecv.at[mine], o_rs.at[mine]).start()
                    pltpu.make_async_copy(ssend.at[mine], srecv.at[mine], s_rs.at[mine]).start()

                @pl.when(x != xk)
                def _():
                    for copy in out_copies(xk, 0):
                        copy.start()
            else:
                for copy in out_copies(xk, dy):
                    copy.start()
        if xk < SIDE - 1:
            lax.fori_loop(SIDE * (xk + 1), PLANE, more, 0)

    for i in range(PLANE):
        pltpu.make_async_copy(srecv.at[i], srecv.at[i], s_rs.at[i]).wait()
    shares = ([], [])
    for h in range(KV_HEADS):
        n0, n1 = SIDE * (h // 2) + 3 * (h % 2), SIDE * (h // 2) + 1 + h % 2
        a, b = srecv[n0], srecv[n1]
        top = jnp.maximum(a, b)
        wa = pltpu.roll(a, 7, 0) * jnp.exp2((a - top) * EXP2_SCALE)
        wb = pltpu.roll(b, 7, 0) * jnp.exp2((b - top) * EXP2_SCALE)
        row = lax.broadcasted_iota(jnp.int32, (8, HEAD_DIM), 0)
        good = (row == 0) | (row == 2)
        wa = jnp.where(good, wa, 1.0)
        wb = jnp.where(good, wb, 1.0)
        both = jnp.maximum(wa + wb, 1e-30)
        shares[0].append(wa / both)
        shares[1].append(wb / both)
    share = jnp.concatenate(shares[0] + shares[1], axis=0).T
    for h in range(KV_HEADS):
        n0, n1 = SIDE * (h // 2) + 3 * (h % 2), SIDE * (h // 2) + 1 + h % 2
        for n in (n0, n1):
            pltpu.make_async_copy(orecv.at[n], orecv.at[n], o_rs.at[n]).wait()
        a, b = orecv[n0].astype(jnp.float32), orecv[n1].astype(jnp.float32)
        for g in range(GROUP):
            part = pl.ds(h * WIDE + g * HEAD_DIM, HEAD_DIM)
            fa = share[:rows, 8 * h + 2 * g:8 * h + 2 * g + 1]
            fb = share[:rows, 64 + 8 * h + 2 * g:64 + 8 * h + 2 * g + 1]
            span = slice(g * HEAD_DIM, (g + 1) * HEAD_DIM)
            out_ref[:, part] = (a[:, span] * fa + b[:, span] * fb).astype(jnp.bfloat16)

    for copy in p_sends + q_sends:
        copy.wait_send()
    for xk in range(SIDE):
        for zk in range(SIDE):
            @pl.when((z < SIDE - 1) & (zk <= z))
            def _():
                z_copy(xk, zk, 1, up_ss).wait_send()

            @pl.when((z > 0) & (zk >= z))
            def _():
                z_copy(xk, zk, -1, dn_ss).wait_send()
        for dy in range(SIDE):
            @pl.when((x != xk) | (dy > 0))
            def _():
                for copy in out_copies(xk, dy):
                    copy.wait_send()


def shards(query_rows, key_rows, value_rows, image_starts, image_counts):
    rows = query_rows.shape[1]
    dma = pltpu.SemaphoreType.DMA
    vmem = pl.BlockSpec(memory_space=pltpu.VMEM)
    smem = pl.BlockSpec(memory_space=pltpu.SMEM)
    out = pl.pallas_call(
        kernel,
        out_shape=jax.ShapeDtypeStruct((rows, HEADS * HEAD_DIM), jnp.bfloat16),
        in_specs=[smem, smem, vmem, vmem, vmem],
        out_specs=vmem,
        scratch_shapes=[
            pltpu.VMEM((PLANE, rows, WIDE), jnp.bfloat16),
            pltpu.VMEM((SIDE, 2, 2, SIDE, rows, HEAD_DIM), jnp.bfloat16),
            pltpu.VMEM((PLANE, rows, HEAD_DIM), jnp.int32),
            pltpu.VMEM((PLANE, GROUP * rows, HEAD_DIM), jnp.float32),
            pltpu.VMEM((PLANE, GROUP * rows, HEAD_DIM), jnp.float32),
            pltpu.VMEM((PLANE, GROUP * rows, HEAD_DIM), jnp.float32),
            pltpu.VMEM((PLANE, rows, WIDE), jnp.bfloat16),
            pltpu.VMEM((PLANE, 8, HEAD_DIM), jnp.float32),
            pltpu.VMEM((PLANE, rows, WIDE), jnp.bfloat16),
            pltpu.VMEM((PLANE, 8, HEAD_DIM), jnp.float32),
            dma((PLANE,)), dma((PLANE,)),
            dma((16,)), dma((2, SIDE, 2)),
            dma((SIDE, SIDE)), dma((SIDE, SIDE)), dma((SIDE, SIDE)),
            dma((SIDE, SIDE)), dma((PLANE,)), dma((SIDE, SIDE)), dma((PLANE,)),
        ],
        compiler_params=pltpu.CompilerParams(collective_id=0, has_side_effects=True, vmem_limit_bytes=56 << 20),
        name="attend",
    )(image_starts, image_counts, query_rows[0], key_rows[0], value_rows[0])
    return out[None]


def solution(mesh):
    return jax.shard_map(
        shards,
        mesh=mesh,
        in_specs=(P("req", "ctx", None), P("req", "ctx", None), P("req", "ctx", None), P("req", None), P("req")),
        out_specs=P("req", "ctx", None),
        check_vma=False,
    )
```

time: 936 us -> 83.5 us (0.09)
  the two profiles are of different devices: /device:TPU:126 before, /device:TPU:6 now
where the time goes in v1:
time: 83.5 us; the launch traced here: 83.3 us
  Pallas kernels  80.8 us (97%)
  local copies, waits for them, and re-layouts  1.82 us (2%)
    pallas_call x1, Pallas kernels, shards(): pl.pallas_call(kernel, out_shape=jax.ShapeDtypeStruct((rows, HEADS * HEAD...  80.8 us
    unnamed x1, local copies, waits for them, and re-layouts  1.82 us

profile of v1, /device:TPU:6, one launch (start us, length us, event | category | flops | bytes accessed | tf_op | source)
XLA Modules:
  0.0 83.3 jit_solution(10442392435704496313)
XLA Ops:
  0.7 80.8 %attend.1 = bf16[112,2048]{1,0:T(8,128)(2,1)} custom-call(s32[1,14]{1,0:T(1,128)} %starts_ref.1, s32[1]{0:T(128)S(6)} %copy.7.count_ref, bf16[112,2048]{1,0:T(8,128)(2,1)} %bitcast.5, bf16[112,1024]{1,0:T(8,128)(2,1)} %bitcast.6, bf16[112,1024]{1,0:T(8,128)(2,1)} %bitcast.7), custom_call_target="tpu_custom_call" | custom-call | tf_op jit(solution)/shard_map/attend/pallas_call | solution.py:292
  81.5 1.8 %copy.8 = bf16[1,112,2048]{2,1,0:T(8,128)(2,1)} copy(bf16[1,112,2048]{2,1,0:T(8,128)(2,1)} %bitcast.4) | data formatting | bytes 917504

commit v2 on v0

v2 whole, which is shorter than its diff:
```python
import math

import jax
import jax.numpy as jnp
from jax import lax
from jax.experimental import pallas as pl
from jax.experimental.pallas import tpu as pltpu
from jax.sharding import PartitionSpec as P

HEADS = 16
KV_HEADS = 8
HEAD_DIM = 128
IMG = 256
SIDE = 4
PLANE = SIDE * SIDE
GROUP = HEADS // KV_HEADS
WIDE = GROUP * HEAD_DIM
BLOCKS = 2 * SIDE
NEG = -1e30
MESH = pl.DeviceIdType.MESH

score_scale = 168.0 ** (-0.5)
EXP2_SCALE = score_scale * math.log2(math.e)

OWN_RIGHT, OWN_LEFT, FAR_RIGHT, FAR_LEFT, PASS_RIGHT, PASS_LEFT = range(6)


def kernel(starts_ref, count_ref, q_ref, k_ref, v_ref, out_ref,
           qg, kv, lim, acc, mx, osend,
           p_ss, p_rs, q_ss, q_rs, c_ss, c_rs, r_ss, r_rs, o_ss, o_rs):
    rows = q_ref.shape[0]
    maximg = starts_ref.shape[1]
    c = lax.axis_index("ctx")
    swap = lax.axis_index("req") % 2
    x, y, z = c // PLANE, (c // SIDE) % SIDE, c % SIDE
    a = x + swap * (y - x)
    s = y + swap * (x - y)
    near = 2 * (z // 2)
    far = 2 - near
    zi = z % 2
    pair = z + 1 - 2 * zi
    outer = (z + z // 2 + 1) % 2
    head = SIDE * outer + a
    is_self = (swap == 0) | (y % 2 == 0)

    def origin(xk):
        return y + swap * ((x - y - xk + 2 * SIDE) % SIDE - y)

    def chip(xx, yy, zz):
        return {"ctx": xx * PLANE + yy * SIDE + zz}

    def beside(step):
        ss = (s + step + SIDE) % SIDE
        return chip(a + swap * (ss - a), ss + swap * (a - ss), z)

    def keeper(aa, zz):
        return chip(aa + swap * ((x + y + aa) % SIDE - aa), y + swap * (aa - y), zz)

    left, right = beside(-1), beside(1)
    mirror = chip(x, y, SIDE - 1 - z)

    barrier = pltpu.get_barrier_semaphore()

    def hello(to):
        pl.semaphore_signal(barrier, inc=1, device_id=to, device_id_type=MESH)

    for d in range(SIDE):
        for zz in (z, pair):
            if d == 0 and zz is z:
                @pl.when(jnp.logical_not(is_self))
                def _():
                    hello(keeper(a, z))
                    hello(chip(x, origin(x), z))
            else:
                hello(keeper((a + d) % SIDE, zz))
                xx = (x + d) % SIDE
                hello(chip(xx, origin(xx), zz))
    for to in (left, right, mirror):
        hello(to)
    pl.semaphore_wait(barrier, 4 * SIDE + 3 - 2 * is_self.astype(jnp.int32))

    def cols(n, width):
        return pl.ds(pl.multiple_of(n * width, width), width)

    def first_copies(d, m, t):
        ta = (a + d) % SIDE
        th = SIDE * ((outer + m) % 2) + ta
        to = keeper(ta, pair if m else z)
        n = (d * 2 + m)
        if t < 2:
            src = (k_ref, v_ref)[t].at[:, cols(th, HEAD_DIM)]
            return src, kv.at[x, t, y, z], p_ss.at[t, n], p_rs.at[t, x, zi], to
        return q_ref.at[:, cols(th, WIDE)], qg.at[2 * x + zi], q_ss.at[n], q_rs.at[2 * x + zi], to

    def remote(src, dst, ss, rs, to):
        return pltpu.make_async_remote_copy(src_ref=src, dst_ref=dst, send_sem=ss, recv_sem=rs, device_id=to,
                                            device_id_type=MESH)

    def first(op, ts):
        for d in range(SIDE):
            for m in (1, 0):
                for t in ts:
                    src, dst, ss, rs, to = first_copies(d, m, t)
                    if d == 0 and m == 0:
                        if op == "start":
                            @pl.when(is_self)
                            def _():
                                pltpu.make_async_copy(src, dst, rs).start()

                        @pl.when(jnp.logical_not(is_self))
                        def _():
                            copy = remote(src, dst, ss, rs, to)
                            copy.start() if op == "start" else copy.wait_send()
                    else:
                        copy = remote(src, dst, ss, rs, to)
                        copy.start() if op == "start" else copy.wait_send()

    first("start", (0, 1))
    first("start", (2,))
    def limits(i, carry):
        pos = ((i // 2) * PLANE + origin(i // 2) * SIDE + near + i % 2) * rows + lax.broadcasted_iota(jnp.int32, (rows, HEAD_DIM), 0)
        slot = pos // IMG * IMG
        found = jnp.zeros((rows, HEAD_DIM), jnp.int32)
        for n in range(maximg):
            begin = jnp.where(n < count_ref[0], starts_ref[0, n], -1)
            found = jnp.where(slot == begin, 1, found)
        lim[i] = jnp.where(found > 0, slot + (IMG - 1), pos)
        mx[i] = jnp.full((GROUP * rows, HEAD_DIM), NEG, jnp.float32)
        acc[i] = jnp.zeros((GROUP * rows, WIDE), jnp.float32)
        return carry

    lax.fori_loop(0, BLOCKS, limits, 0)


    def part(xk, off, half):
        return kv.at[xk, :, (origin(xk) + off + SIDE) % SIDE, pl.ds(half, 2)]

    def cross(xk):
        return remote(part(xk, 0, near), part(xk, 0, near), c_ss.at[xk], c_rs.at[xk], mirror)

    def crossed(xk):
        remote(part(xk, 0, far), part(xk, 0, far), c_ss.at[xk], c_rs.at[xk], mirror).wait_recv()

    sent = {OWN_RIGHT: (0, near, right), OWN_LEFT: (0, near, left), FAR_RIGHT: (0, far, right),
            FAR_LEFT: (0, far, left), PASS_RIGHT: (-1, near, right), PASS_LEFT: (1, far, left)}
    shift = {OWN_RIGHT: -1, OWN_LEFT: 1, FAR_RIGHT: -1, FAR_LEFT: 1, PASS_RIGHT: -1, PASS_LEFT: 1}

    def ring(kind, xk):
        off, half, to = sent[kind]
        ref = part(xk, off, half)
        return remote(ref, ref, r_ss.at[kind, xk], r_rs.at[kind, xk], to)

    def ring_got(kind, xk):
        off, half, to = sent[kind]
        ref = part(xk, off + shift[kind], half)
        remote(ref, ref, r_ss.at[kind, xk], r_rs.at[kind, xk], to).wait_recv()

    for xk in range(SIDE):
        for t in range(2):
            for zz in range(2):
                ref = kv.at[xk, t, origin(xk), near + zz]
                pltpu.make_async_copy(ref, ref, p_rs.at[t, xk, zz]).wait()
        cross(xk).start()
        ring(OWN_RIGHT, xk).start()
        ring(OWN_LEFT, xk).start()

    def pass_own(xk):
        ring_got(OWN_RIGHT, xk)
        ring(PASS_RIGHT, xk).start()

    def send_far(xk):
        crossed(xk)
        ring(FAR_RIGHT, xk).start()
        ring(FAR_LEFT, xk).start()

    def pass_far(xk):
        ring_got(FAR_LEFT, xk)
        ring(PASS_LEFT, xk).start()

    def ready(xk):
        for kind in (OWN_LEFT, FAR_RIGHT, PASS_RIGHT, PASS_LEFT):
            ring_got(kind, xk)

    for xk in range(SIDE):
        pass_own(xk)
    keys = PLANE * rows

    def tile(xk, xq, masked):
        k = kv[xk, 0].reshape(keys, HEAD_DIM)
        v = jnp.concatenate([kv[xk, 1].reshape(keys, HEAD_DIM), jnp.ones((keys, HEAD_DIM), jnp.bfloat16)], axis=1)

        def scores(j):
            q = qg[2 * xq + j]
            q = jnp.concatenate([q[:, :HEAD_DIM], q[:, HEAD_DIM:]], axis=0)
            return lax.dot_general(q, k, (((1,), (1,)), ((), ())), preferred_element_type=jnp.float32)

        def weights(j, sc):
            if masked:
                at = lax.broadcasted_iota(jnp.int32, (1, keys), 1) + xk * keys
                row_lim = lim[2 * xq + j]
                sc = jnp.where(at <= jnp.concatenate([row_lim, row_lim], axis=0)[:, :1], sc, NEG)
            before = mx[2 * xq + j][:, :1]
            top = jnp.maximum(jnp.max(sc, axis=1, keepdims=True), before)
            mx[2 * xq + j] = jnp.broadcast_to(top, (GROUP * rows, HEAD_DIM))
            return jnp.exp2((sc - top) * EXP2_SCALE).astype(jnp.bfloat16), jnp.exp2((before - top) * EXP2_SCALE)

        def add(j, p, shrink):
            total = acc[2 * xq + j] * shrink + jnp.dot(p, v, preferred_element_type=jnp.float32)
            if not masked:
                acc[2 * xq + j] = total
            else:
                o = (total[:, :HEAD_DIM] / total[:, HEAD_DIM:]).astype(jnp.bfloat16)
                osend[2 * xq + j] = jnp.concatenate([o[:rows], o[rows:]], axis=1)

        s0 = scores(0)
        s1 = scores(1)
        p0 = weights(0, s0)
        p1 = weights(1, s1)
        add(0, *p0)
        add(1, *p1)

    def out_copy(op, xq):
        for j in range(2):
            src, dst = osend.at[2 * xq + j], out_ref.at[:, cols(head, WIDE)]
            here = (xq == x) & (origin(xq) == y) & (zi == j)
            if op == "start":
                @pl.when(here)
                def _():
                    pltpu.make_async_copy(src, dst, o_rs.at[head]).start()

            @pl.when(jnp.logical_not(here))
            def _():
                copy = remote(src, dst, o_ss.at[2 * xq + j], o_rs.at[head], chip(xq, origin(xq), near + j))
                copy.start() if op == "start" else copy.wait_send()

    def step(n, carry):
        xk = (n >= 4).astype(jnp.int32) + (n >= 7).astype(jnp.int32) + (n >= 9).astype(jnp.int32)
        xq = n - (4 * xk - xk * (xk - 1) // 2) + xk

        @pl.when(n == 0)
        def _():
            send_far(0)
            send_far(1)
            pass_far(0)
            for i in range(BLOCKS):
                pltpu.make_async_copy(qg.at[i], qg.at[i], q_rs.at[i]).wait()
            ready(0)

        @pl.when(n == 2)
        def _():
            send_far(2)
            pass_far(1)

        @pl.when(n == 4)
        def _():
            ready(1)

        @pl.when(n == 5)
        def _():
            send_far(3)
            pass_far(2)

        @pl.when(n == 6)
        def _():
            pass_far(3)

        @pl.when(n == 7)
        def _():
            ready(2)

        @pl.when(n == 9)
        def _():
            ready(3)

        @pl.when(xq == xk)
        def _():
            tile(xk, xq, True)
            out_copy("start", xq)

        @pl.when(xq != xk)
        def _():
            tile(xk, xq, False)
        return carry

    lax.fori_loop(0, SIDE * (SIDE + 1) // 2, step, 0)

    for h in range(KV_HEADS):
        ref = out_ref.at[:, pl.ds(h * WIDE, WIDE)]
        pltpu.make_async_copy(ref, ref, o_rs.at[h]).wait()
    first("wait", (0, 1, 2))
    for xk in range(SIDE):
        cross(xk).wait_send()
        for kind in range(6):
            ring(kind, xk).wait_send()
        out_copy("wait", xk)


def shards(query_rows, key_rows, value_rows, image_starts, image_counts):
    rows = query_rows.shape[1]
    dma = pltpu.SemaphoreType.DMA
    vmem = pl.BlockSpec(memory_space=pltpu.VMEM)
    smem = pl.BlockSpec(memory_space=pltpu.SMEM)
    out = pl.pallas_call(
        kernel,
        out_shape=jax.ShapeDtypeStruct((rows, HEADS * HEAD_DIM), jnp.bfloat16),
        in_specs=[smem, smem, vmem, vmem, vmem],
        out_specs=vmem,
        scratch_shapes=[
            pltpu.VMEM((BLOCKS, rows, WIDE), jnp.bfloat16),
            pltpu.VMEM((SIDE, 2, SIDE, SIDE, rows, HEAD_DIM), jnp.bfloat16),
            pltpu.VMEM((BLOCKS, rows, HEAD_DIM), jnp.int32),
            pltpu.VMEM((BLOCKS, GROUP * rows, WIDE), jnp.float32),
            pltpu.VMEM((BLOCKS, GROUP * rows, HEAD_DIM), jnp.float32),
            pltpu.VMEM((BLOCKS, rows, WIDE), jnp.bfloat16),
            dma((2, BLOCKS)), dma((2, SIDE, 2)), dma((BLOCKS,)), dma((BLOCKS,)),
            dma((SIDE,)), dma((SIDE,)), dma((6, SIDE)), dma((6, SIDE)), dma((BLOCKS,)), dma((KV_HEADS,)),
        ],
        compiler_params=pltpu.CompilerParams(collective_id=0, has_side_effects=True, vmem_limit_bytes=56 << 20),
        name="attend",
    )(image_starts, image_counts, query_rows[0], key_rows[0], value_rows[0])
    return out[None]


def solution(mesh):
    return jax.shard_map(
        shards,
        mesh=mesh,
        in_specs=(P("req", "ctx", None), P("req", "ctx", None), P("req", "ctx", None), P("req", None), P("req")),
        out_specs=P("req", "ctx", None),
        check_vma=False,
    )
```

time: 936 us -> 67.3 us (0.07)
  the two profiles are of different devices: /device:TPU:126 before, /device:TPU:6 now
where the time goes in v2:
time: 67.3 us; the launch traced here: 67.2 us
  Pallas kernels  64.7 us (96%)
  local copies, waits for them, and re-layouts  1.82 us (3%)
    pallas_call x1, Pallas kernels, shards(): pl.pallas_call(kernel, out_shape=jax.ShapeDtypeStruct((rows, HEADS * HEAD...  64.7 us
    unnamed x1, local copies, waits for them, and re-layouts  1.82 us

profile of v2, /device:TPU:6, one launch (start us, length us, event | category | flops | bytes accessed | tf_op | source)
XLA Modules:
  0.0 67.2 jit_solution(11430651842723555929)
XLA Ops:
  0.7 64.7 %attend.1 = bf16[112,2048]{1,0:T(8,128)(2,1)} custom-call(s32[1,14]{1,0:T(1,128)} %starts_ref.1, s32[1]{0:T(128)S(6)} %copy.7.count_ref, bf16[112,2048]{1,0:T(8,128)(2,1)} %bitcast.5, bf16[112,1024]{1,0:T(8,128)(2,1)} %bitcast.6, bf16[112,1024]{1,0:T(8,128)(2,1)} %bitcast.7), custom_call_target="tpu_custom_call" | custom-call | tf_op jit(solution)/shard_map/attend/pallas_call | solution.py:303
  65.3 1.8 %copy.8 = bf16[1,112,2048]{2,1,0:T(8,128)(2,1)} copy(bf16[1,112,2048]{2,1,0:T(8,128)(2,1)} %bitcast.4) | data formatting | bytes 917504

commit v3 on v2

--- a/solution.py
+++ b/solution.py
@@ -21,8 +21,6 @@
 
 score_scale = 168.0 ** (-0.5)
 EXP2_SCALE = score_scale * math.log2(math.e)
-
-OWN_RIGHT, OWN_LEFT, FAR_RIGHT, FAR_LEFT, PASS_RIGHT, PASS_LEFT = range(6)
 
 
 def kernel(starts_ref, count_ref, q_ref, k_ref, v_ref, out_ref,
@@ -56,7 +54,6 @@
     def keeper(aa, zz):
         return chip(aa + swap * ((x + y + aa) % SIDE - aa), y + swap * (aa - y), zz)
 
-    left, right = beside(-1), beside(1)
     mirror = chip(x, y, SIDE - 1 - z)
 
     barrier = pltpu.get_barrier_semaphore()
@@ -75,9 +72,10 @@
                 hello(keeper((a + d) % SIDE, zz))
                 xx = (x + d) % SIDE
                 hello(chip(xx, origin(xx), zz))
-    for to in (left, right, mirror):
-        hello(to)
-    pl.semaphore_wait(barrier, 4 * SIDE + 3 - 2 * is_self.astype(jnp.int32))
+    for step in range(1, SIDE):
+        hello(beside(step))
+    hello(mirror)
+    pl.semaphore_wait(barrier, 5 * SIDE - 2 * is_self.astype(jnp.int32))
 
     def cols(n, width):
         return pl.ds(pl.multiple_of(n * width, width), width)
@@ -97,7 +95,7 @@
                                             device_id_type=MESH)
 
     def first(op, ts):
-        for d in range(SIDE):
+        for d in (0, 3, 1, 2):
             for m in (1, 0):
                 for t in ts:
                     src, dst, ss, rs, to = first_copies(d, m, t)
@@ -141,49 +139,59 @@
     def crossed(xk):
         remote(part(xk, 0, far), part(xk, 0, far), c_ss.at[xk], c_rs.at[xk], mirror).wait_recv()
 
-    sent = {OWN_RIGHT: (0, near, right), OWN_LEFT: (0, near, left), FAR_RIGHT: (0, far, right),
-            FAR_LEFT: (0, far, left), PASS_RIGHT: (-1, near, right), PASS_LEFT: (1, far, left)}
-    shift = {OWN_RIGHT: -1, OWN_LEFT: 1, FAR_RIGHT: -1, FAR_LEFT: 1, PASS_RIGHT: -1, PASS_LEFT: 1}
-
-    def ring(kind, xk):
-        off, half, to = sent[kind]
-        ref = part(xk, off, half)
-        return remote(ref, ref, r_ss.at[kind, xk], r_rs.at[kind, xk], to)
-
-    def ring_got(kind, xk):
-        off, half, to = sent[kind]
-        ref = part(xk, off + shift[kind], half)
-        remote(ref, ref, r_ss.at[kind, xk], r_rs.at[kind, xk], to).wait_recv()
-
-    for xk in range(SIDE):
+    def ring(xk, side, step):
+        ref = part(xk, 0, far if side else near)
+        n = (xk * 2 + side) * SIDE + step
+        return remote(ref, ref, r_ss.at[n], r_rs.at[n], beside(step))
+
+    def ring_got(xk, side, step):
+        ref = part(xk, SIDE - step, far if side else near)
+        n = (xk * 2 + side) * SIDE + step
+        remote(ref, ref, r_ss.at[n], r_rs.at[n], beside(step)).wait_recv()
+
+    def send_near(xk):
+        for turn in (1, 3, 2):
+            ring(xk, 0, turn).start()
+
+    soon = x + swap * ((x - 2 * y + 2 * SIDE) % SIDE - x)
+
+    def order(i):
+        return soon if i == 0 else i - 1 + (soon <= i - 1).astype(jnp.int32)
+
+    for i in range(SIDE):
+        xk = order(i)
         for t in range(2):
             for zz in range(2):
                 ref = kv.at[xk, t, origin(xk), near + zz]
                 pltpu.make_async_copy(ref, ref, p_rs.at[t, xk, zz]).wait()
         cross(xk).start()
-        ring(OWN_RIGHT, xk).start()
-        ring(OWN_LEFT, xk).start()
-
-    def pass_own(xk):
-        ring_got(OWN_RIGHT, xk)
-        ring(PASS_RIGHT, xk).start()
+        if i < 4:
+            send_near(xk)
 
     def send_far(xk):
         crossed(xk)
-        ring(FAR_RIGHT, xk).start()
-        ring(FAR_LEFT, xk).start()
-
-    def pass_far(xk):
-        ring_got(FAR_LEFT, xk)
-        ring(PASS_LEFT, xk).start()
+        for turn in (1, 3, 2):
+            ring(xk, 1, turn).start()
 
     def ready(xk):
-        for kind in (OWN_LEFT, FAR_RIGHT, PASS_RIGHT, PASS_LEFT):
-            ring_got(kind, xk)
-
-    for xk in range(SIDE):
-        pass_own(xk)
+        for turn in range(1, SIDE):
+            for side in range(2):
+                ring_got(xk, side, turn)
+
     keys = PLANE * rows
+
+    def out_copy(op, xq, j):
+        src, dst = osend.at[2 * xq + j], out_ref.at[:, cols(head, WIDE)]
+        here = (xq == x) & (origin(xq) == y) & (zi == j)
+        if op == "start":
+            @pl.when(here)
+            def _():
+                pltpu.make_async_copy(src, dst, o_rs.at[head]).start()
+
+        @pl.when(jnp.logical_not(here))
+        def _():
+            copy = remote(src, dst, o_ss.at[2 * xq + j], o_rs.at[head], chip(xq, origin(xq), near + j))
+            copy.start() if op == "start" else copy.wait_send()
 
     def tile(xk, xq, masked):
         k = kv[xk, 0].reshape(keys, HEAD_DIM)
@@ -215,23 +223,15 @@
         s0 = scores(0)
         s1 = scores(1)
         p0 = weights(0, s0)
-        p1 = weights(1, s1)
-        add(0, *p0)
-        add(1, *p1)
-
-    def out_copy(op, xq):
-        for j in range(2):
-            src, dst = osend.at[2 * xq + j], out_ref.at[:, cols(head, WIDE)]
-            here = (xq == x) & (origin(xq) == y) & (zi == j)
-            if op == "start":
-                @pl.when(here)
-                def _():
-                    pltpu.make_async_copy(src, dst, o_rs.at[head]).start()
-
-            @pl.when(jnp.logical_not(here))
-            def _():
-                copy = remote(src, dst, o_ss.at[2 * xq + j], o_rs.at[head], chip(xq, origin(xq), near + j))
-                copy.start() if op == "start" else copy.wait_send()
+        if masked:
+            add(0, *p0)
+            out_copy("start", xq, 0)
+            add(1, *weights(1, s1))
+            out_copy("start", xq, 1)
+        else:
+            p1 = weights(1, s1)
+            add(0, *p0)
+            add(1, *p1)
 
     def step(n, carry):
         xk = (n >= 4).astype(jnp.int32) + (n >= 7).astype(jnp.int32) + (n >= 9).astype(jnp.int32)
@@ -239,30 +239,20 @@
 
         @pl.when(n == 0)
         def _():
-            send_far(0)
-            send_far(1)
-            pass_far(0)
+            send_far(order(0))
+            send_far(order(1))
             for i in range(BLOCKS):
                 pltpu.make_async_copy(qg.at[i], qg.at[i], q_rs.at[i]).wait()
             ready(0)
 
-        @pl.when(n == 2)
-        def _():
-            send_far(2)
-            pass_far(1)
+        @pl.when(n == 1)
+        def _():
+            send_far(order(2))
 
         @pl.when(n == 4)
         def _():
             ready(1)
-
-        @pl.when(n == 5)
-        def _():
-            send_far(3)
-            pass_far(2)
-
-        @pl.when(n == 6)
-        def _():
-            pass_far(3)
+            send_far(order(3))
 
         @pl.when(n == 7)
         def _():
@@ -275,7 +265,6 @@
         @pl.when(xq == xk)
         def _():
             tile(xk, xq, True)
-            out_copy("start", xq)
 
         @pl.when(xq != xk)
         def _():
@@ -290,21 +279,23 @@
     first("wait", (0, 1, 2))
     for xk in range(SIDE):
         cross(xk).wait_send()
-        for kind in range(6):
-            ring(kind, xk).wait_send()
-        out_copy("wait", xk)
+        for side in range(2):
+            for turn in range(1, SIDE):
+                ring(xk, side, turn).wait_send()
+        for j in range(2):
+            out_copy("wait", xk, j)
 
 
 def shards(query_rows, key_rows, value_rows, image_starts, image_counts):
     rows = query_rows.shape[1]
     dma = pltpu.SemaphoreType.DMA
-    vmem = pl.BlockSpec(memory_space=pltpu.VMEM)
     smem = pl.BlockSpec(memory_space=pltpu.SMEM)
+    hbm = pl.BlockSpec(memory_space=pltpu.HBM)
     out = pl.pallas_call(
         kernel,
         out_shape=jax.ShapeDtypeStruct((rows, HEADS * HEAD_DIM), jnp.bfloat16),
-        in_specs=[smem, smem, vmem, vmem, vmem],
-        out_specs=vmem,
+        in_specs=[smem, smem, hbm, hbm, hbm],
+        out_specs=hbm,
         scratch_shapes=[
             pltpu.VMEM((BLOCKS, rows, WIDE), jnp.bfloat16),
             pltpu.VMEM((SIDE, 2, SIDE, SIDE, rows, HEAD_DIM), jnp.bfloat16),
@@ -313,7 +304,7 @@
             pltpu.VMEM((BLOCKS, GROUP * rows, HEAD_DIM), jnp.float32),
             pltpu.VMEM((BLOCKS, rows, WIDE), jnp.bfloat16),
             dma((2, BLOCKS)), dma((2, SIDE, 2)), dma((BLOCKS,)), dma((BLOCKS,)),
-            dma((SIDE,)), dma((SIDE,)), dma((6, SIDE)), dma((6, SIDE)), dma((BLOCKS,)), dma((KV_HEADS,)),
+            dma((SIDE,)), dma((SIDE,)), dma((2 * PLANE,)), dma((2 * PLANE,)), dma((BLOCKS,)), dma((KV_HEADS,)),
         ],
         compiler_params=pltpu.CompilerParams(collective_id=0, has_side_effects=True, vmem_limit_bytes=56 << 20),
         name="attend",

time: 67.3 us -> 61.6 us (0.915)
  Pallas kernels: 64.7 us -> 58.9 us
    pallas_call x1, Pallas kernels: 64.7 us -> 58.9 us  [shards(): pl.pallas_call(kernel, out_shape=jax.ShapeDtypeStruct((rows, HEADS * HEAD...]
where the time goes in v3:
time: 61.6 us; the launch traced here: 61.3 us
  Pallas kernels  58.9 us (96%)
  local copies, waits for them, and re-layouts  1.82 us (3%)
  between operations  0.66 us (1%)
    pallas_call x1, Pallas kernels, shards(): pl.pallas_call(kernel, out_shape=jax.ShapeDtypeStruct((rows, HEADS * HEAD...  58.9 us
    unnamed x1, local copies, waits for them, and re-layouts  1.82 us

profile of v3, /device:TPU:6, one launch (start us, length us, event | category | flops | bytes accessed | tf_op | source)
XLA Modules:
  0.0 61.3 jit_solution(8452124969511396391)
XLA Ops:
  0.7 58.9 %attend.1 = bf16[112,2048]{1,0:T(8,128)(2,1)} custom-call(s32[1,14]{1,0:T(1,128)} %starts_ref.1, s32[1]{0:T(128)S(6)} %copy.7.count_ref, bf16[112,2048]{1,0:T(8,128)(2,1)} %bitcast.5, bf16[112,1024]{1,0:T(8,128)(2,1)} %bitcast.6, bf16[112,1024]{1,0:T(8,128)(2,1)} %bitcast.7), custom_call_target="tpu_custom_call" | custom-call | tf_op jit(solution)/shard_map/attend/pallas_call | solution.py:294
  59.5 1.8 %copy.8 = bf16[1,112,2048]{2,1,0:T(8,128)(2,1)} copy(bf16[1,112,2048]{2,1,0:T(8,128)(2,1)} %bitcast.4) | data formatting | bytes 917504

commit v4 on v3

--- a/solution.py
+++ b/solution.py
@@ -193,85 +193,53 @@
             copy = remote(src, dst, o_ss.at[2 * xq + j], o_rs.at[head], chip(xq, origin(xq), near + j))
             copy.start() if op == "start" else copy.wait_send()
 
-    def tile(xk, xq, masked):
+    def scores(xk, i):
+        q = qg[i]
+        q = jnp.concatenate([q[:, :HEAD_DIM], q[:, HEAD_DIM:]], axis=0)
         k = kv[xk, 0].reshape(keys, HEAD_DIM)
+        return lax.dot_general(q, k, (((1,), (1,)), ((), ())), preferred_element_type=jnp.float32)
+
+    def weights(xk, i, sc):
+        if i // 2 == xk:
+            at = lax.broadcasted_iota(jnp.int32, (1, keys), 1) + xk * keys
+            row_lim = lim[i]
+            sc = jnp.where(at <= jnp.concatenate([row_lim, row_lim], axis=0)[:, :1], sc, NEG)
+        before = mx[i][:, :1]
+        top = jnp.maximum(jnp.max(sc, axis=1, keepdims=True), before)
+        mx[i] = jnp.broadcast_to(top, (GROUP * rows, HEAD_DIM))
+        return jnp.exp2((sc - top) * EXP2_SCALE).astype(jnp.bfloat16), jnp.exp2((before - top) * EXP2_SCALE)
+
+    def add(xk, i, p, shrink):
         v = jnp.concatenate([kv[xk, 1].reshape(keys, HEAD_DIM), jnp.ones((keys, HEAD_DIM), jnp.bfloat16)], axis=1)
-
-        def scores(j):
-            q = qg[2 * xq + j]
-            q = jnp.concatenate([q[:, :HEAD_DIM], q[:, HEAD_DIM:]], axis=0)
-            return lax.dot_general(q, k, (((1,), (1,)), ((), ())), preferred_element_type=jnp.float32)
-
-        def weights(j, sc):
-            if masked:
-                at = lax.broadcasted_iota(jnp.int32, (1, keys), 1) + xk * keys
-                row_lim = lim[2 * xq + j]
-                sc = jnp.where(at <= jnp.concatenate([row_lim, row_lim], axis=0)[:, :1], sc, NEG)
-            before = mx[2 * xq + j][:, :1]
-            top = jnp.maximum(jnp.max(sc, axis=1, keepdims=True), before)
-            mx[2 * xq + j] = jnp.broadcast_to(top, (GROUP * rows, HEAD_DIM))
-            return jnp.exp2((sc - top) * EXP2_SCALE).astype(jnp.bfloat16), jnp.exp2((before - top) * EXP2_SCALE)
-
-        def add(j, p, shrink):
-            total = acc[2 * xq + j] * shrink + jnp.dot(p, v, preferred_element_type=jnp.float32)
-            if not masked:
-                acc[2 * xq + j] = total
-            else:
-                o = (total[:, :HEAD_DIM] / total[:, HEAD_DIM:]).astype(jnp.bfloat16)
-                osend[2 * xq + j] = jnp.concatenate([o[:rows], o[rows:]], axis=1)
-
-        s0 = scores(0)
-        s1 = scores(1)
-        p0 = weights(0, s0)
-        if masked:
-            add(0, *p0)
-            out_copy("start", xq, 0)
-            add(1, *weights(1, s1))
-            out_copy("start", xq, 1)
+        total = acc[i] * shrink + jnp.dot(p, v, preferred_element_type=jnp.float32)
+        if i // 2 > xk:
+            acc[i] = total
         else:
-            p1 = weights(1, s1)
-            add(0, *p0)
-            add(1, *p1)
-
-    def step(n, carry):
-        xk = (n >= 4).astype(jnp.int32) + (n >= 7).astype(jnp.int32) + (n >= 9).astype(jnp.int32)
-        xq = n - (4 * xk - xk * (xk - 1) // 2) + xk
-
-        @pl.when(n == 0)
-        def _():
-            send_far(order(0))
-            send_far(order(1))
-            for i in range(BLOCKS):
-                pltpu.make_async_copy(qg.at[i], qg.at[i], q_rs.at[i]).wait()
-            ready(0)
-
-        @pl.when(n == 1)
-        def _():
-            send_far(order(2))
-
-        @pl.when(n == 4)
-        def _():
-            ready(1)
-            send_far(order(3))
-
-        @pl.when(n == 7)
-        def _():
-            ready(2)
-
-        @pl.when(n == 9)
-        def _():
-            ready(3)
-
-        @pl.when(xq == xk)
-        def _():
-            tile(xk, xq, True)
-
-        @pl.when(xq != xk)
-        def _():
-            tile(xk, xq, False)
-        return carry
-
-    lax.fori_loop(0, SIDE * (SIDE + 1) // 2, step, 0)
+            o = (total[:, :HEAD_DIM] / total[:, HEAD_DIM:]).astype(jnp.bfloat16)
+            osend[i] = jnp.concatenate([o[:rows], o[rows:]], axis=1)
+
+    def run(units):
+        sc, held = scores(*units[0]), None
+        for n, unit in enumerate(units):
+            later = scores(*units[n + 1]) if n + 1 < len(units) else None
+            p = weights(*unit, sc)
+            if held is not None:
+                add(*held)
+            held, sc = (*unit, *p), later
+        add(*held)
+
+    def plane(xk):
+        run([(xk, i) for i in range(2 * xk, BLOCKS)])
+        for j in range(2):
+            out_copy("start", xk, j)
+
+    for n in range(SIDE):
+        send_far(order(n))
+    for i in range(BLOCKS):
+        pltpu.make_async_copy(qg.at[i], qg.at[i], q_rs.at[i]).wait()
+    for xk in range(SIDE):
+        ready(xk)
+        plane(xk)
 
     for h in range(KV_HEADS):
         ref = out_ref.at[:, pl.ds(h * WIDE, WIDE)]

time: 61.6 us -> 55.4 us (0.90)
  Pallas kernels: 58.9 us -> 52.6 us
    pallas_call x1, Pallas kernels: 58.9 us -> 52.6 us  [shards(): pl.pallas_call(kernel, out_shape=jax.ShapeDtypeStruct((rows, HEADS * HEAD...]
where the time goes in v4:
time: 55.4 us; the launch traced here: 55 us
  Pallas kernels  52.6 us (95%)
  local copies, waits for them, and re-layouts  1.82 us (3%)
  between operations  0.66 us (1%)
    pallas_call x1, Pallas kernels, shards(): pl.pallas_call(kernel, out_shape=jax.ShapeDtypeStruct((rows, HEADS * HEAD...  52.6 us
    unnamed x1, local copies, waits for them, and re-layouts  1.82 us

profile of v4, /device:TPU:6, one launch (start us, length us, event | category | flops | bytes accessed | tf_op | source)
XLA Modules:
  0.0 55.0 jit_solution(7531970682894179015)
XLA Ops:
  0.7 52.6 %attend.1 = bf16[112,2048]{1,0:T(8,128)(2,1)} custom-call(s32[1,14]{1,0:T(1,128)} %starts_ref.1, s32[1]{0:T(128)S(6)} %copy.7.count_ref, bf16[112,2048]{1,0:T(8,128)(2,1)} %bitcast.5, bf16[112,1024]{1,0:T(8,128)(2,1)} %bitcast.6, bf16[112,1024]{1,0:T(8,128)(2,1)} %bitcast.7), custom_call_target="tpu_custom_call" | custom-call | tf_op jit(solution)/shard_map/attend/pallas_call | solution.py:262
  53.2 1.8 %copy.8 = bf16[1,112,2048]{2,1,0:T(8,128)(2,1)} copy(bf16[1,112,2048]{2,1,0:T(8,128)(2,1)} %bitcast.4) | data formatting | bytes 917504

commit v5 on v4

--- a/solution.py
+++ b/solution.py
@@ -150,7 +150,7 @@
         remote(ref, ref, r_ss.at[n], r_rs.at[n], beside(step)).wait_recv()
 
     def send_near(xk):
-        for turn in (1, 3, 2):
+        for turn in (1, 3):
             ring(xk, 0, turn).start()
 
     soon = x + swap * ((x - 2 * y + 2 * SIDE) % SIDE - x)
@@ -168,6 +168,15 @@
         if i < 4:
             send_near(xk)
 
+    def pass_on(xk):
+        n = xk * 2 * SIDE + 2
+        ref = part(xk, SIDE - 1, near)
+        return remote(ref, ref, r_ss.at[n], r_rs.at[n], beside(1))
+
+    for xk in range(SIDE):
+        ring_got(xk, 0, 1)
+        pass_on(xk).start()
+
     def send_far(xk):
         crossed(xk)
         for turn in (1, 3, 2):
@@ -176,7 +185,8 @@
     def ready(xk):
         for turn in range(1, SIDE):
             for side in range(2):
-                ring_got(xk, side, turn)
+                if side or turn > 1:
+                    ring_got(xk, side, turn)
 
     keys = PLANE * rows
 
@@ -249,7 +259,7 @@
         cross(xk).wait_send()
         for side in range(2):
             for turn in range(1, SIDE):
-                ring(xk, side, turn).wait_send()
+                (ring(xk, side, turn) if side or turn != 2 else pass_on(xk)).wait_send()
         for j in range(2):
             out_copy("wait", xk, j)
 

time: 55.4 us -> 55.1 us (level)
  no operation moved by 1% of the time
where the time goes in v5:
time: 55.1 us; the launch traced here: 55 us
  Pallas kernels  52.5 us (95%)
  local copies, waits for them, and re-layouts  1.82 us (3%)
  between operations  0.66 us (1%)
    pallas_call x1, Pallas kernels, shards(): pl.pallas_call(kernel, out_shape=jax.ShapeDtypeStruct((rows, HEADS * HEAD...  52.5 us
    unnamed x1, local copies, waits for them, and re-layouts  1.82 us

profile of v5, /device:TPU:6, one launch (start us, length us, event | category | flops | bytes accessed | tf_op | source)
XLA Modules:
  0.0 55.0 jit_solution(12725266255259622236)
XLA Ops:
  0.7 52.5 %attend.1 = bf16[112,2048]{1,0:T(8,128)(2,1)} custom-call(s32[1,14]{1,0:T(1,128)} %starts_ref.1, s32[1]{0:T(128)S(6)} %copy.7.count_ref, bf16[112,2048]{1,0:T(8,128)(2,1)} %bitcast.5, bf16[112,1024]{1,0:T(8,128)(2,1)} %bitcast.6, bf16[112,1024]{1,0:T(8,128)(2,1)} %bitcast.7), custom_call_target="tpu_custom_call" | custom-call | tf_op jit(solution)/shard_map/attend/pallas_call | solution.py:272
  53.2 1.8 %copy.8 = bf16[1,112,2048]{2,1,0:T(8,128)(2,1)} copy(bf16[1,112,2048]{2,1,0:T(8,128)(2,1)} %bitcast.4) | data formatting | bytes 917504

commit v6 on v5

--- a/solution.py
+++ b/solution.py
@@ -123,8 +123,6 @@
             begin = jnp.where(n < count_ref[0], starts_ref[0, n], -1)
             found = jnp.where(slot == begin, 1, found)
         lim[i] = jnp.where(found > 0, slot + (IMG - 1), pos)
-        mx[i] = jnp.full((GROUP * rows, HEAD_DIM), NEG, jnp.float32)
-        acc[i] = jnp.zeros((GROUP * rows, WIDE), jnp.float32)
         return carry
 
     lax.fori_loop(0, BLOCKS, limits, 0)
@@ -214,14 +212,19 @@
             at = lax.broadcasted_iota(jnp.int32, (1, keys), 1) + xk * keys
             row_lim = lim[i]
             sc = jnp.where(at <= jnp.concatenate([row_lim, row_lim], axis=0)[:, :1], sc, NEG)
-        before = mx[i][:, :1]
-        top = jnp.maximum(jnp.max(sc, axis=1, keepdims=True), before)
+        top = jnp.max(sc, axis=1, keepdims=True)
+        if xk > 0:
+            before = mx[i][:, :1]
+            top = jnp.maximum(top, before)
         mx[i] = jnp.broadcast_to(top, (GROUP * rows, HEAD_DIM))
-        return jnp.exp2((sc - top) * EXP2_SCALE).astype(jnp.bfloat16), jnp.exp2((before - top) * EXP2_SCALE)
+        p = jnp.exp2((sc - top) * EXP2_SCALE).astype(jnp.bfloat16)
+        return p, (jnp.exp2((before - top) * EXP2_SCALE) if xk > 0 else None)
 
     def add(xk, i, p, shrink):
         v = jnp.concatenate([kv[xk, 1].reshape(keys, HEAD_DIM), jnp.ones((keys, HEAD_DIM), jnp.bfloat16)], axis=1)
-        total = acc[i] * shrink + jnp.dot(p, v, preferred_element_type=jnp.float32)
+        total = jnp.dot(p, v, preferred_element_type=jnp.float32)
+        if xk > 0:
+            total = acc[i] * shrink + total
         if i // 2 > xk:
             acc[i] = total
         else:

time: 55.1 us -> 55.1 us (level)
  no operation moved by 1% of the time
where the time goes in v6:
time: 55.1 us; the launch traced here: 55 us
  Pallas kernels  52.5 us (95%)
  local copies, waits for them, and re-layouts  1.82 us (3%)
  between operations  0.66 us (1%)
    pallas_call x1, Pallas kernels, shards(): pl.pallas_call(kernel, out_shape=jax.ShapeDtypeStruct((rows, HEADS * HEAD...  52.5 us
    unnamed x1, local copies, waits for them, and re-layouts  1.82 us

profile of v6, /device:TPU:6, one launch (start us, length us, event | category | flops | bytes accessed | tf_op | source)
XLA Modules:
  0.0 55.0 jit_solution(12423512006483095581)
XLA Ops:
  0.7 52.5 %attend.1 = bf16[112,2048]{1,0:T(8,128)(2,1)} custom-call(s32[1,14]{1,0:T(1,128)} %starts_ref.1, s32[1]{0:T(128)S(6)} %copy.7.count_ref, bf16[112,2048]{1,0:T(8,128)(2,1)} %bitcast.5, bf16[112,1024]{1,0:T(8,128)(2,1)} %bitcast.6, bf16[112,1024]{1,0:T(8,128)(2,1)} %bitcast.7), custom_call_target="tpu_custom_call" | custom-call | tf_op jit(solution)/shard_map/attend/pallas_call | solution.py:275
  53.1 1.8 %copy.8 = bf16[1,112,2048]{2,1,0:T(8,128)(2,1)} copy(bf16[1,112,2048]{2,1,0:T(8,128)(2,1)} %bitcast.4) | data formatting | bytes 917504
